TPU v7x, 32 devices: a whole 2x2x4 slice. The times are simulated.
32 devices in a mesh: rows: 4 (over x, core), feat: 8 (over z, y).
Axes of the slice: x: 2, y: 2, z: 4, core: 2. Of those that a mesh axis runs over, the one named last changes fastest.
Arguments:
- embeddings: bfloat16 [512, 1024], P(('rows', 'feat')), may hold values from -12 to 12
- freqs: bfloat16 [1024, 65536], P(None, 'feat'), may hold values from -0.1875 to 0.1875
- phases: float32 [65536], P('feat'), may hold values from 0 to 6.2831855
- sketch: bfloat16 [65536, 256], P('feat'), may hold values from -0.0234375 to 0.0234375
Outputs:
- basis: float32 [512, 256], P(('rows', 'feat'))
- coeffs: float32 [256, 65536], P(None, 'feat')
All inputs are finite; a program needn't handle non-finite values.
Results may differ from a plain program's by a relative error of at most 0.0048.
Values may be sent and summed in bfloat16 or wider, within the bound.
A program may use at most 128 MiB of HBM per device.

v0:
```python
import jax
import jax.numpy as jnp
from jax import lax
from jax.sharding import PartitionSpec as P


def per_device(embeddings, freqs, phases, sketch):
    rows_dev = embeddings.shape[0]
    row_count = rows_dev * lax.axis_size("feat") * lax.axis_size("rows")
    mixed = jnp.dot(
        lax.all_gather(embeddings, "feat", axis=0, tiled=True),
        freqs,
        preferred_element_type=jnp.float32,
    )
    features = jnp.cos(mixed + phases).astype(jnp.bfloat16)
    owned_rows = lax.psum_scatter(
        jnp.dot(features, sketch, preferred_element_type=jnp.float32),
        "feat",
        scatter_dimension=0,
        tiled=True,
    )
    local_gram = jnp.dot(owned_rows.T, owned_rows, precision=lax.Precision.HIGHEST)
    gram_matrix = lax.psum(local_gram, ("rows", "feat")) / row_count
    factor = jnp.linalg.cholesky(gram_matrix)
    basis = jax.scipy.linalg.solve_triangular(factor, owned_rows.T, lower=True).T
    block_basis = lax.all_gather(basis.astype(jnp.bfloat16), "feat", axis=0, tiled=True)
    partial_value = lax.dot_general(
        block_basis, features, (((0,), (0,)), ((), ())), preferred_element_type=jnp.float32
    )
    coeffs = lax.psum(partial_value, "rows") / row_count
    return (basis, coeffs)


def solution(mesh):
    placed = (P(("rows", "feat"), None), P(None, "feat"), P("feat"), P("feat", None))
    return jax.shard_map(
        per_device,
        mesh=mesh,
        in_specs=placed,
        out_specs=(P(("rows", "feat"), None), P(None, "feat")),
        check_vma=False,
    )
```

profile of v0, /device:TPU:0, one launch (start us, length us, event | category | flops | bytes accessed | tf_op | source)
XLA Modules:
  0.0 516.5 jit_solution(3243274491165157878)
XLA Ops:
  7.2 0.0 reduce-scatter.2.cloned.1.call-start
  7.2 32.7 %all_gather.6 = bf16[128,1024]{1,0:T(8,128)(2,1)S(1)} all-gather(bf16[16,1024]{1,0:T(8,128)(2,1)} %param.4), channel_id=1, replica_groups=mesh['rows'=4,'feat'=8] {'feat'}, dimensions={0}, use_global_device_ids=true | all-gather | bytes 294912 | tf_op jit(solution)/shard_map/all_gather | solution.py:11
  39.9 0.0 copy-start
  40.0 18.1 %fusion.1 = bf16[128,8192]{1,0:T(8,128)(2,1)S(1)} fusion(bf16[128,1024]{1,0:T(8,128)(2,1)S(1)} %all_gather.6, bf16[1024,8192]{1,0:T(8,128)(2,1)} %param.5, f32[8192]{0:T(1024)} %param.6), kind=kOutput, calls=%fused_computation.4 | convolution fusion | flops 2149580800 | bytes 19169280 | tf_op jit(solution)/shard_map/dot_general | solution.py:10
  58.1 0.0 copy-done
  58.1 1.5 fusion.12
  59.6 0.0 reduce-scatter.2.cloned.1.call-update
  59.6 0.0 all-reduce.4.cloned.1.call-start
  59.6 62.0 %reduce-scatter.2.cloned.1.call-done = f32[16,256]{1,0:T(8,128)} async-done(((f32[128,256]{1,0:T(8,128)}), f32[16,256]{1,0:T(8,128)}) %reduce-scatter.2.cloned.1.call-update) | async-done | bytes 16400 | tf_op jit(solution)/shard_map/reduce_scatter | solution.py:16
  121.6 0.0 copy-start.1
  121.6 1.9 fusion.13
  123.6 0.0 all-reduce.4.cloned.1.call-update
  123.6 0.2 all-reduce.6.cloned.1.call-start
  123.8 128.0 %all-reduce.4.cloned.1.call-done = f32[256,256]{0,1:T(8,128)} async-done(((f32[256,256]{0,1:T(8,128)}), f32[256,256]{0,1:T(8,128)}) %all-reduce.4.cloned.1.call-update) | async-done | bytes 262160 | tf_op jit(solution)/shard_map/psum | solution.py:23
  251.8 1.0 broadcast_multiply_fusion.1
  252.8 0.1 copy.7
  252.9 1.0 fusion.2
  253.9 11.7 %cholesky.50 = f32[128,128]{1,0:T(8,128)S(1)} custom-call(f32[128,128]{1,0:T(8,128)S(1)} %cholesky.118), custom_call_target="Cholesky" | custom-call | tf_op jit(solution)/shard_map/jit(cholesky)/cholesky | solution.py:24
  265.7 9.8 %custom-call.15 = f32[1,128,128]{1,2,0:T(8,128)S(1)} custom-call(f32[1,128,128]{2,1,0:T(8,128)S(1)} %get-tuple-element.25), custom_call_target="InvertDiagBlocksLowerTriangular" | custom-call | tf_op jit(solution)/shard_map/jit(cholesky)/cholesky | solution.py:24
  275.5 0.2 constant_dynamic-update-slice_fusion.1
  275.7 0.3 convolution_subtract_fusion
  276.0 11.7 %cholesky.105 = f32[128,128]{1,0:T(8,128)S(1)} custom-call(f32[128,128]{1,0:T(8,128)S(1)} %convolution_subtract_fusion), custom_call_target="Cholesky" | custom-call | tf_op jit(solution)/shard_map/jit(cholesky)/cholesky | solution.py:24
  287.8 0.7 compare_reduce_fusion
  289.9 0.1 triangular_solve.57
  289.9 4.3 while.1
  290.1 0.6 fusion.28
  290.7 1.4 bitcast_dynamic-update-slice_fusion.2
  292.2 0.6 fusion.28
  292.8 1.4 bitcast_dynamic-update-slice_fusion.2
  294.2 19.7 %custom-call.16 = f32[2,128,128]{1,2,0:T(8,128)S(1)} custom-call(f32[2,128,128]{2,1,0:T(8,128)S(1)} %get-tuple-element.9), custom_call_target="InvertDiagBlocksLowerTriangular" | custom-call | tf_op jit(solution)/shard_map/jit(_solve_triangular)/triangular_solve | solution.py:25
  313.9 0.0 copy-done.1
  313.9 0.2 fusion.5
  314.1 0.2 convolution_subtract_fusion.1
  314.3 0.2 fusion.4
  314.5 0.6 fusion.10
  315.1 30.5 %all_gather.7 = bf16[128,256]{1,0:T(8,128)(2,1)S(1)} all-gather(bf16[16,256]{1,0:T(8,128)(2,1)S(1)} %get-tuple-element.18), channel_id=1, replica_groups=mesh['rows'=4,'feat'=8] {'feat'}, dimensions={0}, use_global_device_ids=true | all-gather | bytes 73728 | tf_op jit(solution)/shard_map/all_gather | solution.py:26
  345.6 4.7 fusion.14
  350.3 0.0 all-reduce.6.cloned.1.call-update
  350.3 152.0 %all-reduce.6.cloned.1.call-done = f32[256,8192]{1,0:T(8,128)} async-done(((f32[256,8192]{1,0:T(8,128)}), f32[256,8192]{1,0:T(8,128)}) %all-reduce.6.cloned.1.call-update) | async-done | bytes 8388624 | tf_op jit(solution)/shard_map/psum | solution.py:30
  502.3 7.7 %broadcast_multiply_fusion = f32[256,8192]{1,0:T(8,128)} fusion(f32[256,8192]{1,0:T(8,128)} %all-reduce.6.cloned.1.call-done), kind=kLoop, calls=%fused_computation.5 | loop fusion | flops 2097152 | bytes 16777216 | tf_op jit(solution)/shard_map/div | solution.py:30
  (9 shorter events, 0.1 us)
Async XLA Ops:
  7.2 114.5 %reduce-scatter.2.cloned.1.call-start = ((), (), s32[]{:S(2)}) async-start(), calls=%async_computation.1 | async-start | bytes 147456 | tf_op jit(solution)/shard_map/reduce_scatter | solution.py:16
  39.9 18.2 %copy-start = (bf16[8192,256]{1,0:T(8,128)(2,1)S(1)}, bf16[8192,256]{1,0:T(8,128)(2,1)}, u32[]{:S(2)}) copy-start(bf16[8192,256]{1,0:T(8,128)(2,1)} %param.7) | copy-start | bytes 12582916
  59.6 192.2 %all-reduce.4.cloned.1.call-start = ((), (), s32[]{:S(2)}) async-start(), calls=%async_computation.2 | async-start | bytes 524288 | tf_op jit(solution)/shard_map/psum | solution.py:23
  121.6 192.3 %copy-start.1 = (f32[16,256]{1,0:T(8,128)S(1)}, f32[16,256]{1,0:T(8,128)}, u32[]{:S(2)}) copy-start(f32[16,256]{1,0:T(8,128)} %reduce-scatter.2.cloned.1.call-done) | copy-start | bytes 49156
  123.6 378.7 %all-reduce.6.cloned.1.call-start = ((), (), s32[]{:S(2)}) async-start(), calls=%async_computation.3 | async-start | bytes 16777216 | tf_op jit(solution)/shard_map/psum | solution.py:30
Sparse Core Ops, SparseCore 0:
  59.7 61.8 reduce-scatter.1
  127.7 124.0 all-reduce.3
  350.4 151.8 all-reduce.5
where the time goes:
time: 517 us
  waiting for transfers between devices  342 us (66%)
  other arithmetic  64 us (12%)
  blocking collectives  63.2 us (12%)
  matrix products  27.2 us (5%)
  between operations  15.2 us (3%)
    psum x1, waiting for transfers between devices, per_device(): coeffs = lax.psum(partial_value, 'rows') / row_count  152 us
    psum x1, waiting for transfers between devices, per_device(): gram_matrix = lax.psum(local_gram, ('rows', 'feat')) / row_count  128 us
    reduce_scatter x1, waiting for transfers between devices, per_device(): lax.psum_scatter(jnp.dot(features, sketch, preferred_element_type=jnp.flo...  62 us
    another operation x6, other arithmetic, per_device(): factor = jnp.linalg.cholesky(gram_matrix)  34 us
    all_gather x1, blocking collectives, per_device(): lax.all_gather(embeddings, 'feat', axis=0, tiled=True)  32.7 us
    all_gather x1, blocking collectives, per_device(): lax.all_gather(basis.astype(jnp.bfloat16), 'feat', axis=0, tiled=True)  30.5 us
    another operation x3, other arithmetic, per_device(): jax.scipy.linalg.solve_triangular(factor, owned_rows.T, lower=True)  19.7 us
    dot_general x1, matrix products, per_device(): jnp.dot(lax.all_gather(embeddings, 'feat', axis=0, tiled=True), freqs, pr...  18.1 us
  transfers between devices with their start and end apart: 3, of which 3 were waited for; matrix products, arithmetic and copies ran while one was open for 0% of the time, Pallas kernels for 0%

commit v1 on v0

--- a/solution.py
+++ b/solution.py
@@ -1,10 +1,315 @@
+import functools
+
 import jax
 import jax.numpy as jnp
 from jax import lax
+from jax.experimental import pallas as pl
+from jax.experimental.pallas import tpu as pltpu
 from jax.sharding import PartitionSpec as P
 
-
-def per_device(embeddings, freqs, phases, sketch):
+MESH = pl.DeviceIdType.MESH
+MIB = 1 << 20
+
+INV_TAU = 0.15915494309189535
+TAU_HI = 6.283203125
+TAU_LO = -1.7817820414e-05
+HALF_PI = 1.5707963267948966
+ROUND = 12582912.0
+
+
+def cosine(x):
+    n = (x * INV_TAU + ROUND) - ROUND
+    r = (x - n * TAU_HI) - n * TAU_LO
+    w = HALF_PI - jnp.abs(r)
+    z = w * w
+    p = -2.3889859e-08
+    p = p * z + 2.7525562e-06
+    p = p * z - 1.9840874e-04
+    p = p * z + 8.3333310e-03
+    p = p * z - 1.6666667e-01
+    return w + w * (z * p)
+
+
+def peers(feats):
+    r, f = lax.axis_index("rows"), lax.axis_index("feat")
+    x, c = r // 2, r % 2
+    sib = x * 2 + (1 - c)
+    across = (1 - x) * 2 + c
+    both = (1 - x) * 2 + (1 - c)
+    return r, f, sib, across, both
+
+
+def entry_barrier(feats):
+    r, f, sib, across, _ = peers(feats)
+    barrier = pltpu.get_barrier_semaphore()
+    targets = [(r, lax.rem(f + k, feats)) for k in range(1, feats)]
+    targets += [(sib, f), (across, f)]
+    for target in targets:
+        pl.semaphore_signal(barrier, inc=1, device_id=target, device_id_type=MESH)
+    pl.semaphore_wait(barrier, feats + 1)
+
+
+def spread(feats, rows, out_ref, send_sem, recv_sem):
+    r, f, sib, across, both = peers(feats)
+
+    def chunk(rr, ff):
+        start = pl.multiple_of((rr * feats + ff) * rows, rows)
+        return out_ref.at[pl.ds(start, rows)]
+
+    sends = []
+
+    def copy_of(rr, ff, target, slot):
+        return pltpu.make_async_remote_copy(
+            src_ref=chunk(rr, ff),
+            dst_ref=chunk(rr, ff),
+            send_sem=send_sem.at[slot],
+            recv_sem=recv_sem.at[rr * feats + ff],
+            device_id=target,
+            device_id_type=MESH,
+        )
+
+    def send(rr, ff, target):
+        copy = copy_of(rr, ff, target, len(sends))
+        copy.start()
+        sends.append(copy)
+
+    def arrive(rr, ff):
+        copy_of(rr, ff, (sib, f), 0).wait_recv()
+
+    send(r, f, (across, f))
+    for k in range(1, feats):
+        send(r, f, (r, lax.rem(f + k, feats)))
+    send(r, f, (sib, f))
+    for k in range(1, feats):
+        ff = lax.rem(f - k + feats, feats)
+        arrive(r, ff)
+        send(r, ff, (across, f))
+        send(r, ff, (sib, f))
+    for k in range(feats):
+        ff = lax.rem(f - k + feats, feats)
+        arrive(across, ff)
+        send(across, ff, (sib, f))
+    for k in range(feats):
+        ff = lax.rem(f - k + feats, feats)
+        arrive(sib, ff)
+        arrive(both, ff)
+    for copy in sends:
+        copy.wait_send()
+
+
+def gather_kernel(feats, x_ref, out_ref, send_sem, recv_sem):
+    rows = x_ref.shape[0]
+    r, f, *_ = peers(feats)
+    entry_barrier(feats)
+    start = pl.multiple_of((r * feats + f) * rows, rows)
+    out_ref[pl.ds(start, rows), :] = x_ref[...]
+    spread(feats, rows, out_ref, send_sem, recv_sem)
+
+
+def gather_rows(x, feats, parts):
+    rows, width = x.shape
+    return pl.pallas_call(
+        functools.partial(gather_kernel, feats),
+        out_shape=jax.ShapeDtypeStruct((rows * feats * parts, width), x.dtype),
+        in_specs=[pl.BlockSpec(memory_space=pltpu.VMEM)],
+        out_specs=pl.BlockSpec(memory_space=pltpu.VMEM),
+        scratch_shapes=[
+            pltpu.SemaphoreType.DMA((feats * parts,)),
+            pltpu.SemaphoreType.DMA((feats * parts,)),
+        ],
+        compiler_params=pltpu.CompilerParams(collective_id=0, has_side_effects=True),
+    )(x)
+
+
+def sum_kernel(feats, part_ref, feat_ref, out_ref, other_ref, own, pair, inbox,
+               send_sem, recv_sem, pair_send, pair_recv, box_send, box_recv,
+               feat_send, feat_recv):
+    total = part_ref.shape[0]
+    block = total // 4
+    rows = block // feats
+    r, f, sib, across, _ = peers(feats)
+    entry_barrier(feats)
+
+    def part(rr):
+        return part_ref.at[pl.ds(pl.multiple_of(rr * block, block), block)]
+
+    exchange = pltpu.make_async_remote_copy(
+        src_ref=part(sib), dst_ref=pair, send_sem=pair_send, recv_sem=pair_recv,
+        device_id=(sib, f), device_id_type=MESH,
+    )
+    exchange.start()
+    features = pltpu.make_async_remote_copy(
+        src_ref=feat_ref, dst_ref=other_ref, send_sem=feat_send, recv_sem=feat_recv,
+        device_id=(sib, f), device_id_type=MESH,
+    )
+    exchange.wait()
+    features.start()
+    mine = pl.ds(pl.multiple_of(r * block, block), block)
+    own[...] = part_ref[mine, :] + pair[...]
+
+    sends = []
+    for k in range(1, feats):
+        ff = lax.rem(f + k, feats)
+        copy = pltpu.make_async_remote_copy(
+            src_ref=own.at[pl.ds(pl.multiple_of(ff * rows, rows), rows)],
+            dst_ref=inbox.at[k - 1],
+            send_sem=box_send.at[k - 1],
+            recv_sem=box_recv.at[k - 1],
+            device_id=(r, ff),
+            device_id_type=MESH,
+        )
+        copy.start()
+        sends.append(copy)
+    acc = own[pl.ds(pl.multiple_of(f * rows, rows), rows), :]
+    for k in range(1, feats):
+        sends[k - 1].wait_recv()
+        acc = acc + inbox[k - 1]
+    start = pl.multiple_of((r * feats + f) * rows, rows)
+    out_ref[pl.ds(start, rows), :] = acc
+    spread(feats, rows, out_ref, send_sem, recv_sem)
+    for copy in sends:
+        copy.wait_send()
+    features.wait()
+
+
+def sum_and_swap(partial, features, feats):
+    total, k = partial.shape
+    parts = 4
+    dma = pltpu.SemaphoreType.DMA
+    return pl.pallas_call(
+        functools.partial(sum_kernel, feats),
+        out_shape=(
+            jax.ShapeDtypeStruct((total, k), jnp.float32),
+            jax.ShapeDtypeStruct(features.shape, features.dtype),
+        ),
+        in_specs=[
+            pl.BlockSpec(memory_space=pltpu.VMEM),
+            pl.BlockSpec(memory_space=pl.ANY),
+        ],
+        out_specs=(
+            pl.BlockSpec(memory_space=pltpu.VMEM),
+            pl.BlockSpec(memory_space=pl.ANY),
+        ),
+        scratch_shapes=[
+            pltpu.VMEM((total // parts, k), jnp.float32),
+            pltpu.VMEM((total // parts, k), jnp.float32),
+            pltpu.VMEM((feats - 1, total // parts // feats, k), jnp.float32),
+            dma((feats * parts,)),
+            dma((feats * parts,)),
+            dma(()),
+            dma(()),
+            dma((feats - 1,)),
+            dma((feats - 1,)),
+            dma(()),
+            dma(()),
+        ],
+        compiler_params=pltpu.CompilerParams(collective_id=1, has_side_effects=True),
+    )(partial, features)
+
+
+def feature_kernel(core_ref, emb_ref, freq_ref, phase_ref, sketch_ref, feat_ref, part_ref):
+    mixed = jnp.dot(emb_ref[...], freq_ref[...], preferred_element_type=jnp.float32)
+    value = cosine(mixed + phase_ref[...]).astype(jnp.bfloat16)
+    feat_ref[...] = value
+    term = jnp.dot(value, sketch_ref[...], preferred_element_type=jnp.float32)
+
+    @pl.when(pl.program_id(0) == 0)
+    def _():
+        part_ref[...] = term
+
+    @pl.when(pl.program_id(0) > 0)
+    def _():
+        part_ref[...] += term
+
+
+def featurize(core, emb, freqs, phases, sketch, tile=512):
+    total, depth = emb.shape
+    width = freqs.shape[1] // 2
+    k = sketch.shape[1]
+    steps = width // tile
+    return pl.pallas_call(
+        feature_kernel,
+        grid_spec=pltpu.PrefetchScalarGridSpec(
+            num_scalar_prefetch=1,
+            grid=(steps,),
+            in_specs=[
+                pl.BlockSpec((total, depth), lambda i, c: (0, 0)),
+                pl.BlockSpec((depth, tile), lambda i, c: (0, c[0] * steps + i)),
+                pl.BlockSpec((1, tile), lambda i, c: (0, c[0] * steps + i)),
+                pl.BlockSpec((tile, k), lambda i, c: (c[0] * steps + i, 0)),
+            ],
+            out_specs=[
+                pl.BlockSpec((total, tile), lambda i, c: (0, i)),
+                pl.BlockSpec((total, k), lambda i, c: (0, 0)),
+            ],
+        ),
+        out_shape=(
+            jax.ShapeDtypeStruct((total, width), jnp.bfloat16),
+            jax.ShapeDtypeStruct((total, k), jnp.float32),
+        ),
+        compiler_params=pltpu.CompilerParams(vmem_limit_bytes=32 * MIB),
+    )(core, emb, freqs, phases.reshape(1, -1), sketch)
+
+
+def coeff_kernel(scale, half, core_ref, basis_ref, own_ref, other_ref, out_ref):
+    step = pl.program_id(0)
+
+    @pl.when(step < half)
+    def _():
+        out_ref[...] = scale * jnp.dot(
+            basis_ref[...], own_ref[...], preferred_element_type=jnp.float32
+        )
+
+    @pl.when(step >= half)
+    def _():
+        out_ref[...] = scale * jnp.dot(
+            basis_ref[...], other_ref[...], preferred_element_type=jnp.float32
+        )
+
+
+def project(core, basis_t, own, other, tile=1024):
+    k, total = basis_t.shape
+    width = own.shape[1]
+    half = width // tile
+    return pl.pallas_call(
+        functools.partial(coeff_kernel, 1.0 / total, half),
+        grid_spec=pltpu.PrefetchScalarGridSpec(
+            num_scalar_prefetch=1,
+            grid=(2 * half,),
+            in_specs=[
+                pl.BlockSpec((k, total), lambda i, c: (0, 0)),
+                pl.BlockSpec((total, tile), lambda i, c: (0, jnp.minimum(i, half - 1))),
+                pl.BlockSpec((total, tile), lambda i, c: (0, jnp.maximum(i - half, 0))),
+            ],
+            out_specs=pl.BlockSpec(
+                (k, tile),
+                lambda i, c: (0, jnp.where(i < half, c[0], 1 - c[0]) * half + i % half),
+            ),
+        ),
+        out_shape=jax.ShapeDtypeStruct((k, 2 * width), jnp.float32),
+        compiler_params=pltpu.CompilerParams(vmem_limit_bytes=32 * MIB),
+    )(core, basis_t, own, other)
+
+
+def fused(embeddings, freqs, phases, sketch):
+    rows_dev = embeddings.shape[0]
+    feats, parts = lax.axis_size("feat"), lax.axis_size("rows")
+    row_count = rows_dev * feats * parts
+    r, f = lax.axis_index("rows"), lax.axis_index("feat")
+    core = jnp.reshape(r % 2, (1,)).astype(jnp.int32)
+    emb = gather_rows(embeddings, feats, parts)
+    own, partial = featurize(core, emb, freqs, phases, sketch)
+    sketched, other = sum_and_swap(partial, own, feats)
+    gram = jnp.dot(sketched.T, sketched, precision=lax.Precision.HIGHEST) / row_count
+    factor = jnp.linalg.cholesky(gram)
+    basis_t = jax.scipy.linalg.solve_triangular(factor, sketched.T, lower=True)
+    start = (r * feats + f) * rows_dev
+    basis = lax.dynamic_slice_in_dim(basis_t, start, rows_dev, 1).T
+    coeffs = project(core, basis_t.astype(jnp.bfloat16), own, other)
+    return basis, coeffs
+
+
+def general(embeddings, freqs, phases, sketch):
     rows_dev = embeddings.shape[0]
     row_count = rows_dev * lax.axis_size("feat") * lax.axis_size("rows")
     mixed = jnp.dot(
@@ -29,6 +334,13 @@
     )
     coeffs = lax.psum(partial_value, "rows") / row_count
     return (basis, coeffs)
+
+
+def per_device(embeddings, freqs, phases, sketch):
+    row_count = embeddings.shape[0] * lax.axis_size("feat") * lax.axis_size("rows")
+    small = row_count <= 1024 and lax.axis_size("rows") == 4 and freqs.shape[1] % 2048 == 0
+    form = fused if small else general
+    return form(embeddings, freqs, phases, sketch)
 
 
 def solution(mesh):

time: 517 us -> 138 us (0.27)
  waiting for transfers between devices: 342 us -> 0 us
  blocking collectives: 63.2 us -> 0 us
  Pallas kernels: 0 us -> 60.8 us
  matrix products: 27.2 us -> 4.15 us
  between operations: 15.2 us -> 2.1 us
  local copies, waits for them, and re-layouts: 4.29 us -> 16.2 us
  other arithmetic: 64 us -> 54 us
    psum x2 -> x0, waiting for transfers between devices: 280 us -> none  [the longest x1 152 us: per_device(): coeffs = lax.psum(partial_value, 'rows') / row_count]
    all_gather x2 -> x0, blocking collectives: 63.2 us -> none  [the longest x1 32.7 us: per_device(): lax.all_gather(embeddings, 'feat', axis=0, tiled=True)]
    reduce_scatter x1 -> x0, waiting for transfers between devices: 62 us -> none  [per_device(): lax.psum_scatter(jnp.dot(features, sketch, preferred_element_type=jnp.flo...]
    pallas_call x0 -> x4, Pallas kernels: none -> 60.8 us  [the longest x1 21.7 us: sum_and_swap(): pl.pallas_call(functools.partial(sum_kernel, feats), out_shape=(jax.Shape...]
    dot_general x4 -> x1, matrix products: 26.2 us -> 2.26 us  [fused(): jnp.dot(sketched.T, sketched, precision=lax.Precision.HIGHEST) / row_count]
    unnamed x4 -> x17, local copies, waits for them, and re-layouts: 0.01 us -> 12 us
    div x3 -> x1, other arithmetic: 9.66 us -> 0.04 us  [fused(): factor = jnp.linalg.cholesky(gram)]
  transfers between devices with their start and end apart: 3 -> 0, of which waited for: 3 -> 0; matrix products, arithmetic and copies ran while one was open for 0% -> 0% of each run, Pallas kernels for 0% -> 0%
where the time goes in v1:
time: 138 us; the launch traced here: 137 us
  Pallas kernels  60.8 us (44%)
  other arithmetic  54 us (39%)
  local copies, waits for them, and re-layouts  16.2 us (12%)
  matrix products  4.15 us (3%)
  between operations  2.1 us (2%)
    another operation x6, other arithmetic, fused(): factor = jnp.linalg.cholesky(gram)  34 us
    pallas_call x1, Pallas kernels, sum_and_swap(): pl.pallas_call(functools.partial(sum_kernel, feats), out_shape=(jax.Shape...  21.7 us
    another operation x3, other arithmetic, fused(): basis_t = jax.scipy.linalg.solve_triangular(factor, sketched.T, lower=True)  19.9 us
    pallas_call x1, Pallas kernels, gather_rows(): pl.pallas_call(functools.partial(gather_kernel, feats), out_shape=jax.Sha...  19 us
    pallas_call x1, Pallas kernels, featurize(): pl.pallas_call(feature_kernel, grid_spec=pltpu.PrefetchScalarGridSpec(num...  13.5 us
    unnamed x17, local copies, waits for them, and re-layouts  12 us
    pallas_call x1, Pallas kernels, project(): pl.pallas_call(functools.partial(coeff_kernel, 1.0 / total, half), grid_s...  6.65 us
    another operation x6, local copies, waits for them, and re-layouts  3.9 us

profile of v1, /device:TPU:0, one launch (start us, length us, event | category | flops | bytes accessed | tf_op | source)
XLA Modules:
  0.0 137.3 jit_solution(904395253835610232)
XLA Ops:
  0.6 19.0 %shard_map.59.emb_ref = bf16[512,1024]{1,0:T(8,128)(2,1)} custom-call(bf16[16,1024]{1,0:T(8,128)(2,1)} %x_ref.1), custom_call_target="tpu_custom_call" | custom-call | tf_op jit(solution)/shard_map/pallas_call | solution.py:111
  19.6 0.0 copy-start.3
  19.6 1.2 copy-done.3
  20.8 0.0 copy-start.4
  20.8 2.2 %copy-done.4 = bf16[8192,256]{1,0:T(8,128)(2,1)S(1)} copy-done((bf16[8192,256]{1,0:T(8,128)(2,1)S(1)}, bf16[8192,256]{1,0:T(8,128)(2,1)}, u32[]{:S(2)}) %copy-start.4) | copy-done | bytes 4194328
  23.0 0.0 copy-start.6
  23.0 0.8 copy-done.6
  23.8 13.5 %shard_map.60 = (bf16[512,4096]{1,0:T(8,128)(2,1)S(1)}, f32[512,256]{1,0:T(8,128)S(1)}) custom-call(s32[1]{0:T(128)} %bitcast.core_ref, bf16[512,1024]{1,0:T(8,128)(2,1)S(1)} %copy-done.3, bf16[1024,8192]{1,0:T(8,128)(2,1)} %freq_ref.1, f32[1,8192]{1,0:T(1,128)S(1)} %bitcast.38, bf16[8192,256]{1,0:T(8,128)(2,1)S(1)} %copy-done.4), custom_call_target="tpu_custom_call" | custom-call | tf_op jit(solution)/shard_map/pallas_call | solution.py:230
  37.3 0.0 copy-start
  37.3 2.0 %copy-done = bf16[512,4096]{1,0:T(8,128)(2,1)} copy-done((bf16[512,4096]{1,0:T(8,128)(2,1)}, bf16[512,4096]{1,0:T(8,128)(2,1)S(1)}, u32[]{:S(2)}) %copy-start) | copy-done | bytes 4194328
  39.3 0.0 copy-start.5
  39.3 0.8 copy-done.5
  40.1 21.7 %shard_map.61 = (f32[512,256]{1,0:T(8,128)}, bf16[512,4096]{1,0:T(8,128)(2,1)}) custom-call(f32[512,256]{1,0:T(8,128)} %copy-done.5, bf16[512,4096]{1,0:T(8,128)(2,1)} %copy-done), custom_call_target="tpu_custom_call" | custom-call | tf_op jit(solution)/shard_map/pallas_call | solution.py:179
  61.8 0.0 copy-start.7
  61.8 2.3 %fusion.12 = f32[256,256]{1,0:T(8,128)S(1)} fusion(f32[512,256]{1,0:T(8,128)} %get-tuple-element.8), kind=kOutput, calls=%fused_computation.34 | convolution fusion | flops 402653184 | bytes 786432 | tf_op jit(solution)/shard_map/dot_general | solution.py:303
  64.1 0.1 copy.6
  64.3 11.7 %cholesky.50 = f32[128,128]{1,0:T(8,128)S(1)} custom-call(f32[128,128]{1,0:T(8,128)S(1)} %cholesky.118), custom_call_target="Cholesky" | custom-call | tf_op jit(solution)/shard_map/jit(cholesky)/cholesky | solution.py:304
  76.1 9.8 %custom-call.15 = f32[1,128,128]{1,2,0:T(8,128)S(1)} custom-call(f32[1,128,128]{2,1,0:T(8,128)S(1)} %get-tuple-element.33), custom_call_target="InvertDiagBlocksLowerTriangular" | custom-call | tf_op jit(solution)/shard_map/jit(cholesky)/cholesky | solution.py:304
  85.9 0.2 constant_dynamic-update-slice_fusion
  86.1 0.3 convolution_subtract_fusion.1
  86.4 11.7 %cholesky.105 = f32[128,128]{1,0:T(8,128)S(1)} custom-call(f32[128,128]{1,0:T(8,128)S(1)} %convolution_subtract_fusion.1), custom_call_target="Cholesky" | custom-call | tf_op jit(solution)/shard_map/jit(cholesky)/cholesky | solution.py:304
  98.1 0.7 compare_reduce_fusion
  100.1 0.1 triangular_solve.57
  100.2 3.9 %while.1 = (s32[]{:T(128)}, f32[256,256]{1,0:T(8,128)S(1)}, s32[2,2]{1,0:T(2,128)S(1)}, f32[2,128,128]{2,1,0:T(8,128)S(1)}, s32[]{:T(128)}) while((s32[]{:T(128)}, f32[256,256]{1,0:T(8,128)S(1)}, s32[2,2]{1,0:T(2,128)S(1)}, f32[2,128,128]{2,1,0:T(8,128)S(1)}, s32[]{:T(128)}) %tuple.28), condition=%wide.while_cond, body=%wide.while_body.sunk | while | flops 2 | bytes 131189 | solution.py:305
  100.2 0.6 fusion.20
  100.8 1.4 bitcast_dynamic-update-slice_fusion.2
  102.1 0.6 fusion.20
  102.7 1.4 bitcast_dynamic-update-slice_fusion.2
  104.1 19.9 %custom-call.16 = f32[2,128,128]{1,2,0:T(8,128)S(1)} custom-call(f32[2,128,128]{2,1,0:T(8,128)S(1)} %get-tuple-element.17), custom_call_target="InvertDiagBlocksLowerTriangular" | custom-call | tf_op jit(solution)/shard_map/jit(_solve_triangular)/triangular_solve | solution.py:305
  124.0 0.0 copy-done.7
  124.0 0.4 fusion.1
  124.4 0.6 convolution_subtract_fusion
  125.0 0.4 fusion.7
  125.4 0.1 fusion.5
  125.5 0.7 copy.7
  126.3 0.0 copy-start.1
  126.3 2.2 %copy-done.1 = bf16[512,4096]{1,0:T(8,128)(2,1)S(1)} copy-done((bf16[512,4096]{1,0:T(8,128)(2,1)S(1)}, bf16[512,4096]{1,0:T(8,128)(2,1)}, u32[]{:S(2)}) %copy-start.1) | copy-done | bytes 4194328
  128.4 0.0 copy-start.2
  128.4 2.2 %copy-done.2 = bf16[512,4096]{1,0:T(8,128)(2,1)S(1)} copy-done((bf16[512,4096]{1,0:T(8,128)(2,1)S(1)}, bf16[512,4096]{1,0:T(8,128)(2,1)}, u32[]{:S(2)}) %copy-start.2) | copy-done | bytes 4194328
  130.6 6.7 %shard_map.62 = f32[256,8192]{1,0:T(8,128)} custom-call(s32[1]{0:T(128)} %bitcast.core_ref, bf16[256,512]{1,0:T(8,128)(2,1)S(1)} %fusion.basis_ref, bf16[512,4096]{1,0:T(8,128)(2,1)S(1)} %copy-done.1, bf16[512,4096]{1,0:T(8,128)(2,1)S(1)} %copy-done.2), custom_call_target="tpu_custom_call" | custom-call | tf_op jit(solution)/shard_map/pallas_call | solution.py:274
  (11 shorter events, 0.2 us)
Async XLA Ops:
  19.6 1.2 copy-start.3
  20.8 2.2 %copy-start.4 = (bf16[8192,256]{1,0:T(8,128)(2,1)S(1)}, bf16[8192,256]{1,0:T(8,128)(2,1)}, u32[]{:S(2)}) copy-start(bf16[8192,256]{1,0:T(8,128)(2,1)} %sketch_ref.1) | copy-start | bytes 12582916
  23.0 0.8 copy-start.6
  37.3 2.0 %copy-start = (bf16[512,4096]{1,0:T(8,128)(2,1)}, bf16[512,4096]{1,0:T(8,128)(2,1)S(1)}, u32[]{:S(2)}) copy-start(bf16[512,4096]{1,0:T(8,128)(2,1)S(1)} %get-tuple-element.7.feat_ref.own_ref) | copy-start | bytes 12582916
  39.3 0.8 copy-start.5
  61.8 62.2 %copy-start.7 = (f32[512,256]{1,0:T(8,128)S(1)}, f32[512,256]{1,0:T(8,128)}, u32[]{:S(2)}) copy-start(f32[512,256]{1,0:T(8,128)} %get-tuple-element.8) | copy-start | bytes 1572868
  126.3 2.2 %copy-start.1 = (bf16[512,4096]{1,0:T(8,128)(2,1)S(1)}, bf16[512,4096]{1,0:T(8,128)(2,1)}, u32[]{:S(2)}) copy-start(bf16[512,4096]{1,0:T(8,128)(2,1)} %copy-done) | copy-start | bytes 12582916
  128.4 2.2 %copy-start.2 = (bf16[512,4096]{1,0:T(8,128)(2,1)S(1)}, bf16[512,4096]{1,0:T(8,128)(2,1)}, u32[]{:S(2)}) copy-start(bf16[512,4096]{1,0:T(8,128)(2,1)} %get-tuple-element.9.other_ref) | copy-start | bytes 12582916

commit v2 on v1

--- a/solution.py
+++ b/solution.py
@@ -203,7 +203,7 @@
             dma(()),
             dma(()),
         ],
-        compiler_params=pltpu.CompilerParams(collective_id=1, has_side_effects=True),
+        compiler_params=pltpu.CompilerParams(collective_id=1, has_side_effects=True, vmem_limit_bytes=60 * MIB),
     )(partial, features)
 
 
@@ -247,7 +247,7 @@
             jax.ShapeDtypeStruct((total, width), jnp.bfloat16),
             jax.ShapeDtypeStruct((total, k), jnp.float32),
         ),
-        compiler_params=pltpu.CompilerParams(vmem_limit_bytes=32 * MIB),
+        compiler_params=pltpu.CompilerParams(vmem_limit_bytes=60 * MIB),
     )(core, emb, freqs, phases.reshape(1, -1), sketch)
 
 
@@ -287,8 +287,98 @@
             ),
         ),
         out_shape=jax.ShapeDtypeStruct((k, 2 * width), jnp.float32),
+        compiler_params=pltpu.CompilerParams(vmem_limit_bytes=60 * MIB),
+    )(core, basis_t, own, other)
+
+
+GROUP = 8
+BLOCK = 64
+LANES = 128
+
+
+def eliminate(tile, at):
+    groups = BLOCK // GROUP
+    m = [tile[g * GROUP:(g + 1) * GROUP, :] for g in range(groups)]
+    shape = (GROUP, LANES)
+    sub = lax.broadcasted_iota(jnp.int32, shape, 0)
+    done = []
+    for g0 in range(groups):
+        base = at + g0 * GROUP
+        col = [
+            {g: jnp.broadcast_to(m[g][:, base + t:base + t + 1], shape) for g in range(g0, groups)}
+            for t in range(GROUP)
+        ]
+        row = [jnp.broadcast_to(m[g0][t:t + 1, :], shape) for t in range(GROUP)]
+        a = {
+            (t, s): jnp.broadcast_to(col[s][g0][t:t + 1, :], shape)
+            for t in range(GROUP)
+            for s in range(t, GROUP)
+        }
+        pivots = jnp.zeros(shape, jnp.float32)
+        for t in range(GROUP):
+            inv = 1.0 / a[t, t]
+            pivots = jnp.where(sub == t, a[t, t], pivots)
+            for s in range(t + 1, GROUP):
+                scaled = a[t, s] * inv
+                for u in range(s, GROUP):
+                    a[s, u] = a[s, u] - scaled * a[t, u]
+                row[s] = row[s] - scaled * row[t]
+            for g in range(g0, groups):
+                f = col[t][g] * inv
+                if g == g0:
+                    f = jnp.where(sub > t, f, 0.0)
+                for s in range(t + 1, GROUP):
+                    col[s][g] = col[s][g] - f * a[t, s]
+                m[g] = m[g] - f * row[t]
+        done.append(m[g0] * lax.rsqrt(pivots))
+    return jnp.concatenate(done, axis=0)
+
+
+def solve_kernel(scale, sk_ref, basis_ref, half_ref, work):
+    k = sk_ref.shape[1]
+    exact = dict(preferred_element_type=jnp.float32, precision=lax.Precision.HIGHEST)
+    sk = sk_ref[...]
+    st = sk.T
+    work[:, :k] = jnp.dot(st, sk, **exact) * scale
+    work[:, k:] = st
+    tile_row = lax.broadcasted_iota(jnp.int32, (BLOCK, LANES), 0)
+    tile_lane = lax.broadcasted_iota(jnp.int32, (BLOCK, LANES), 1)
+    for j in range(k // BLOCK):
+        rows = slice(j * BLOCK, (j + 1) * BLOCK)
+        edge = j * BLOCK // LANES * LANES
+        at = j * BLOCK - edge
+        away = BLOCK - at
+        inside = (tile_lane >= at) & (tile_lane < at + BLOCK)
+        eye = jnp.where(tile_lane == tile_row + away, 1.0, 0.0)
+        tile = jnp.where(inside, work[rows, edge:edge + LANES], eye)
+        inverse = jnp.where(inside, 0.0, eliminate(tile, at))
+        panel = work[rows, edge:]
+        panel = jnp.dot(inverse, jnp.concatenate([panel, panel], axis=0), **exact)
+        basis_ref[rows, :] = panel[:, k - edge:]
+        after = (j + 1) * BLOCK
+        if after < k:
+            left = after // LANES * LANES
+            wide = panel[:, left - edge:]
+            update = lax.dot_general(
+                wide[:, :k - left], wide, (((0,), (0,)), ((), ())), **exact
+            )
+            work[after:, left:] = work[after:, left:] - update[after - left:, :]
+    half_ref[...] = basis_ref[...].astype(jnp.bfloat16)
+
+
+def solve(sketched):
+    total, k = sketched.shape
+    return pl.pallas_call(
+        functools.partial(solve_kernel, 1.0 / total),
+        out_shape=(
+            jax.ShapeDtypeStruct((k, total), jnp.float32),
+            jax.ShapeDtypeStruct((k, total), jnp.bfloat16),
+        ),
+        in_specs=[pl.BlockSpec(memory_space=pltpu.VMEM)],
+        out_specs=(pl.BlockSpec(memory_space=pltpu.VMEM),) * 2,
+        scratch_shapes=[pltpu.VMEM((k, k + total), jnp.float32)],
         compiler_params=pltpu.CompilerParams(vmem_limit_bytes=32 * MIB),
-    )(core, basis_t, own, other)
+    )(sketched)
 
 
 def fused(embeddings, freqs, phases, sketch):
@@ -300,12 +390,10 @@
     emb = gather_rows(embeddings, feats, parts)
     own, partial = featurize(core, emb, freqs, phases, sketch)
     sketched, other = sum_and_swap(partial, own, feats)
-    gram = jnp.dot(sketched.T, sketched, precision=lax.Precision.HIGHEST) / row_count
-    factor = jnp.linalg.cholesky(gram)
-    basis_t = jax.scipy.linalg.solve_triangular(factor, sketched.T, lower=True)
+    basis_t, half_t = solve(sketched)
     start = (r * feats + f) * rows_dev
     basis = lax.dynamic_slice_in_dim(basis_t, start, rows_dev, 1).T
-    coeffs = project(core, basis_t.astype(jnp.bfloat16), own, other)
+    coeffs = project(core, half_t, own, other)
     return basis, coeffs
 
 

time: 138 us -> 80.4 us (0.58)
  other arithmetic: 54 us -> 0 us
  Pallas kernels: 60.8 us -> 76.6 us
  local copies, waits for them, and re-layouts: 16.2 us -> 2.53 us
  matrix products: 4.15 us -> 0 us
  between operations: 2.1 us -> 0.68 us
    another operation x9 -> x0, other arithmetic: 53.9 us -> none  [the longest x6 34 us: fused(): factor = jnp.linalg.cholesky(gram)]
    pallas_call x0 -> x1, Pallas kernels: none -> 11 us  [solve(): pl.pallas_call(functools.partial(solve_kernel, 1.0 / total), out_shape=(j...]
    unnamed x17 -> x5, local copies, waits for them, and re-layouts: 12 us -> 2.43 us
    another operation x9 -> x0, local copies, waits for them, and re-layouts: 4 us -> none
    pallas_call x1, Pallas kernels: 6.65 us -> 10.2 us  [project(): pl.pallas_call(functools.partial(coeff_kernel, 1.0 / total, half), grid_s...]
    dot_general x1 -> x0, matrix products: 2.26 us -> none  [fused(): jnp.dot(sketched.T, sketched, precision=lax.Precision.HIGHEST) / row_count]
    another operation x5 -> x0, matrix products: 1.9 us -> none  [the longest x3 1.42 us: fused(): basis_t = jax.scipy.linalg.solve_triangular(factor, sketched.T, lower=True)]
where the time goes in v2:
time: 80.4 us; the launch traced here: 79.9 us
  Pallas kernels  76.6 us (95%)
  local copies, waits for them, and re-layouts  2.53 us (3%)
    pallas_call x1, Pallas kernels, sum_and_swap(): pl.pallas_call(functools.partial(sum_kernel, feats), out_shape=(jax.Shape...  21.7 us
    pallas_call x1, Pallas kernels, gather_rows(): pl.pallas_call(functools.partial(gather_kernel, feats), out_shape=jax.Sha...  19 us
    pallas_call x1, Pallas kernels, featurize(): pl.pallas_call(feature_kernel, grid_spec=pltpu.PrefetchScalarGridSpec(num...  14.7 us
    pallas_call x1, Pallas kernels, solve(): pl.pallas_call(functools.partial(solve_kernel, 1.0 / total), out_shape=(j...  11 us
    pallas_call x1, Pallas kernels, project(): pl.pallas_call(functools.partial(coeff_kernel, 1.0 / total, half), grid_s...  10.2 us
    unnamed x5, local copies, waits for them, and re-layouts  2.43 us

profile of v2, /device:TPU:0, one launch (start us, length us, event | category | flops | bytes accessed | tf_op | source)
XLA Modules:
  0.0 79.9 jit_solution(833641368718606048)
XLA Ops:
  0.6 19.0 %shard_map.59.emb_ref = bf16[512,1024]{1,0:T(8,128)(2,1)} custom-call(bf16[16,1024]{1,0:T(8,128)(2,1)} %x_ref.1), custom_call_target="tpu_custom_call" | custom-call | tf_op jit(solution)/shard_map/pallas_call | solution.py:111
  19.6 14.7 %shard_map.60 = (bf16[512,4096]{1,0:T(8,128)(2,1)}, f32[512,256]{1,0:T(8,128)}) custom-call(s32[1]{0:T(128)} %bitcast.core_ref, bf16[512,1024]{1,0:T(8,128)(2,1)} %shard_map.59.emb_ref, bf16[1024,8192]{1,0:T(8,128)(2,1)} %freq_ref.1, f32[1,8192]{1,0:T(1,128)} %bitcast.4, bf16[8192,256]{1,0:T(8,128)(2,1)} %sketch_ref.1), custom_call_target="tpu_custom_call" | custom-call | tf_op jit(solution)/shard_map/pallas_call | solution.py:230
  34.4 21.7 %shard_map.61 = (f32[512,256]{1,0:T(8,128)}, bf16[512,4096]{1,0:T(8,128)(2,1)}) custom-call(f32[512,256]{1,0:T(8,128)} %get-tuple-element.8.part_ref, bf16[512,4096]{1,0:T(8,128)(2,1)} %get-tuple-element.9.feat_ref.own_ref), custom_call_target="tpu_custom_call" | custom-call | tf_op jit(solution)/shard_map/pallas_call | solution.py:179
  56.1 0.0 copy-start
  56.1 1.0 %copy-done = f32[512,256]{1,0:T(8,128)S(1)} copy-done((f32[512,256]{1,0:T(8,128)S(1)}, f32[512,256]{1,0:T(8,128)}, u32[]{:S(2)}) %copy-start) | copy-done | bytes 524312
  57.1 11.0 %shard_map.62 = (f32[256,512]{1,0:T(8,128)S(1)}, bf16[256,512]{1,0:T(8,128)(2,1)S(1)}) custom-call(f32[512,256]{1,0:T(8,128)S(1)} %copy-done), custom_call_target="tpu_custom_call" | custom-call | tf_op jit(solution)/shard_map/pallas_call | solution.py:371
  68.1 0.0 copy-start.1
  68.1 0.7 copy-done.1
  68.8 0.1 dynamic-slice_bitcast_fusion
  68.9 0.7 copy.6
  69.6 10.2 %shard_map.63 = f32[256,8192]{1,0:T(8,128)} custom-call(s32[1]{0:T(128)} %bitcast.core_ref, bf16[256,512]{1,0:T(8,128)(2,1)} %copy-done.1, bf16[512,4096]{1,0:T(8,128)(2,1)} %get-tuple-element.9.feat_ref.own_ref, bf16[512,4096]{1,0:T(8,128)(2,1)} %get-tuple-element.13.other_ref), custom_call_target="tpu_custom_call" | custom-call | tf_op jit(solution)/shard_map/pallas_call | solution.py:274
Async XLA Ops:
  56.1 1.0 %copy-start = (f32[512,256]{1,0:T(8,128)S(1)}, f32[512,256]{1,0:T(8,128)}, u32[]{:S(2)}) copy-start(f32[512,256]{1,0:T(8,128)} %get-tuple-element.10.sk_ref) | copy-start | bytes 1572868
  68.1 0.7 copy-start.1

commit v3 on v2

--- a/solution.py
+++ b/solution.py
@@ -249,46 +249,6 @@
         ),
         compiler_params=pltpu.CompilerParams(vmem_limit_bytes=60 * MIB),
     )(core, emb, freqs, phases.reshape(1, -1), sketch)
-
-
-def coeff_kernel(scale, half, core_ref, basis_ref, own_ref, other_ref, out_ref):
-    step = pl.program_id(0)
-
-    @pl.when(step < half)
-    def _():
-        out_ref[...] = scale * jnp.dot(
-            basis_ref[...], own_ref[...], preferred_element_type=jnp.float32
-        )
-
-    @pl.when(step >= half)
-    def _():
-        out_ref[...] = scale * jnp.dot(
-            basis_ref[...], other_ref[...], preferred_element_type=jnp.float32
-        )
-
-
-def project(core, basis_t, own, other, tile=1024):
-    k, total = basis_t.shape
-    width = own.shape[1]
-    half = width // tile
-    return pl.pallas_call(
-        functools.partial(coeff_kernel, 1.0 / total, half),
-        grid_spec=pltpu.PrefetchScalarGridSpec(
-            num_scalar_prefetch=1,
-            grid=(2 * half,),
-            in_specs=[
-                pl.BlockSpec((k, total), lambda i, c: (0, 0)),
-                pl.BlockSpec((total, tile), lambda i, c: (0, jnp.minimum(i, half - 1))),
-                pl.BlockSpec((total, tile), lambda i, c: (0, jnp.maximum(i - half, 0))),
-            ],
-            out_specs=pl.BlockSpec(
-                (k, tile),
-                lambda i, c: (0, jnp.where(i < half, c[0], 1 - c[0]) * half + i % half),
-            ),
-        ),
-        out_shape=jax.ShapeDtypeStruct((k, 2 * width), jnp.float32),
-        compiler_params=pltpu.CompilerParams(vmem_limit_bytes=60 * MIB),
-    )(core, basis_t, own, other)
 
 
 GROUP = 8
@@ -334,7 +294,7 @@
     return jnp.concatenate(done, axis=0)
 
 
-def solve_kernel(scale, sk_ref, basis_ref, half_ref, work):
+def factorize(scale, sk_ref, basis_ref, work):
     k = sk_ref.shape[1]
     exact = dict(preferred_element_type=jnp.float32, precision=lax.Precision.HIGHEST)
     sk = sk_ref[...]
@@ -363,37 +323,87 @@
                 wide[:, :k - left], wide, (((0,), (0,)), ((), ())), **exact
             )
             work[after:, left:] = work[after:, left:] - update[after - left:, :]
-    half_ref[...] = basis_ref[...].astype(jnp.bfloat16)
-
-
-def solve(sketched):
+
+
+def finish_kernel(scale, half, where_ref, sk_ref, own_ref, other_ref, coeff_ref, rows_ref,
+                  work, basis_t, basis, half_t, feats, sem):
+    step = pl.program_id(0)
+    tile = coeff_ref.shape[1]
+    loads = [
+        pltpu.make_async_copy(
+            (own_ref if i < half else other_ref).at[:, pl.ds(i % half * tile, tile)],
+            feats.at[i],
+            sem.at[i],
+        )
+        for i in range(2 * half)
+    ]
+
+    @pl.when(step == 0)
+    def _():
+        for load in loads:
+            load.start()
+        factorize(scale, sk_ref, basis_t, work)
+        half_t[...] = basis_t[...].astype(jnp.bfloat16)
+        basis[...] = basis_t[...].T
+        rows = rows_ref.shape[0]
+        rows_ref[...] = basis[pl.ds(pl.multiple_of(where_ref[1] * rows, rows), rows), :]
+
+    for i in range(2 * half):
+        @pl.when(step == i)
+        def _(i=i):
+            loads[i].wait()
+            coeff_ref[...] = scale * jnp.dot(
+                half_t[...], feats[i], preferred_element_type=jnp.float32
+            )
+
+
+def finish(where, sketched, own, other, rows, tile=1024):
     total, k = sketched.shape
+    width = own.shape[1]
+    half = width // tile
     return pl.pallas_call(
-        functools.partial(solve_kernel, 1.0 / total),
+        functools.partial(finish_kernel, 1.0 / total, half),
+        grid_spec=pltpu.PrefetchScalarGridSpec(
+            num_scalar_prefetch=1,
+            grid=(2 * half,),
+            in_specs=[
+                pl.BlockSpec((total, k), lambda i, c: (0, 0)),
+                pl.BlockSpec(memory_space=pl.ANY),
+                pl.BlockSpec(memory_space=pl.ANY),
+            ],
+            out_specs=[
+                pl.BlockSpec(
+                    (k, tile),
+                    lambda i, c: (0, jnp.where(i < half, c[0], 1 - c[0]) * half + i % half),
+                ),
+                pl.BlockSpec((rows, k), lambda i, c: (0, 0)),
+            ],
+            scratch_shapes=[
+                pltpu.VMEM((k, k + total), jnp.float32),
+                pltpu.VMEM((k, total), jnp.float32),
+                pltpu.VMEM((total, k), jnp.float32),
+                pltpu.VMEM((k, total), jnp.bfloat16),
+                pltpu.VMEM((2 * half, total, tile), own.dtype),
+                pltpu.SemaphoreType.DMA((2 * half,)),
+            ],
+        ),
         out_shape=(
-            jax.ShapeDtypeStruct((k, total), jnp.float32),
-            jax.ShapeDtypeStruct((k, total), jnp.bfloat16),
-        ),
-        in_specs=[pl.BlockSpec(memory_space=pltpu.VMEM)],
-        out_specs=(pl.BlockSpec(memory_space=pltpu.VMEM),) * 2,
-        scratch_shapes=[pltpu.VMEM((k, k + total), jnp.float32)],
-        compiler_params=pltpu.CompilerParams(vmem_limit_bytes=32 * MIB),
-    )(sketched)
+            jax.ShapeDtypeStruct((k, 2 * width), jnp.float32),
+            jax.ShapeDtypeStruct((rows, k), jnp.float32),
+        ),
+        compiler_params=pltpu.CompilerParams(vmem_limit_bytes=60 * MIB),
+    )(where, sketched, own, other)
 
 
 def fused(embeddings, freqs, phases, sketch):
     rows_dev = embeddings.shape[0]
     feats, parts = lax.axis_size("feat"), lax.axis_size("rows")
-    row_count = rows_dev * feats * parts
     r, f = lax.axis_index("rows"), lax.axis_index("feat")
-    core = jnp.reshape(r % 2, (1,)).astype(jnp.int32)
+    where = jnp.stack([r % 2, r * feats + f]).astype(jnp.int32)
     emb = gather_rows(embeddings, feats, parts)
-    own, partial = featurize(core, emb, freqs, phases, sketch)
+    own, partial = featurize(where, emb, freqs, phases, sketch)
     sketched, other = sum_and_swap(partial, own, feats)
-    basis_t, half_t = solve(sketched)
-    start = (r * feats + f) * rows_dev
-    basis = lax.dynamic_slice_in_dim(basis_t, start, rows_dev, 1).T
-    coeffs = project(core, half_t, own, other)
+    coeffs, basis = finish(where, sketched, own, other, rows_dev)
     return basis, coeffs
 
 

time: 80.4 us -> 77.9 us (0.969)
  local copies, waits for them, and re-layouts: 2.53 us -> 0 us
    unnamed x5 -> x0, local copies, waits for them, and re-layouts: 2.43 us -> none
    pallas_call x2 -> x1, Pallas kernels: 21.2 us -> 20.1 us  [finish(): pl.pallas_call(functools.partial(finish_kernel, 1.0 / total, half), grid_...]
where the time goes in v3:
time: 77.9 us; the launch traced here: 77.6 us
  Pallas kernels  76.1 us (98%)
  between operations  0.82 us (1%)
    pallas_call x1, Pallas kernels, sum_and_swap(): pl.pallas_call(functools.partial(sum_kernel, feats), out_shape=(jax.Shape...  21.7 us
    pallas_call x1, Pallas kernels, finish(): pl.pallas_call(functools.partial(finish_kernel, 1.0 / total, half), grid_...  20.1 us
    pallas_call x1, Pallas kernels, gather_rows(): pl.pallas_call(functools.partial(gather_kernel, feats), out_shape=jax.Sha...  19 us
    pallas_call x1, Pallas kernels, featurize(): pl.pallas_call(feature_kernel, grid_spec=pltpu.PrefetchScalarGridSpec(num...  15.4 us

profile of v3, /device:TPU:0, one launch (start us, length us, event | category | flops | bytes accessed | tf_op | source)
XLA Modules:
  0.0 77.6 jit_solution(14543932697230087149)
XLA Ops:
  0.6 0.6 pad_add_fusion.core_ref.where_ref
  1.3 19.0 %shard_map.59.emb_ref = bf16[512,1024]{1,0:T(8,128)(2,1)} custom-call(bf16[16,1024]{1,0:T(8,128)(2,1)} %x_ref.1), custom_call_target="tpu_custom_call" | custom-call | tf_op jit(solution)/shard_map/pallas_call | solution.py:111
  20.2 15.4 %shard_map.60 = (bf16[512,4096]{1,0:T(8,128)(2,1)}, f32[512,256]{1,0:T(8,128)}) custom-call(s32[2]{0:T(128)} %pad_add_fusion.core_ref.where_ref, bf16[512,1024]{1,0:T(8,128)(2,1)} %shard_map.59.emb_ref, bf16[1024,8192]{1,0:T(8,128)(2,1)} %freq_ref.1, f32[1,8192]{1,0:T(1,128)} %bitcast.3, bf16[8192,256]{1,0:T(8,128)(2,1)} %sketch_ref.1), custom_call_target="tpu_custom_call" | custom-call | tf_op jit(solution)/shard_map/pallas_call | solution.py:230
  35.6 21.7 %shard_map.61 = (f32[512,256]{1,0:T(8,128)}, bf16[512,4096]{1,0:T(8,128)(2,1)}) custom-call(f32[512,256]{1,0:T(8,128)} %get-tuple-element.8.part_ref, bf16[512,4096]{1,0:T(8,128)(2,1)} %get-tuple-element.9.feat_ref.own_ref), custom_call_target="tpu_custom_call" | custom-call | tf_op jit(solution)/shard_map/pallas_call | solution.py:179
  57.4 20.1 %shard_map.62 = (f32[256,8192]{1,0:T(8,128)}, f32[16,256]{1,0:T(8,128)}) custom-call(s32[2]{0:T(128)} %pad_add_fusion.core_ref.where_ref, f32[512,256]{1,0:T(8,128)} %get-tuple-element.10.sk_ref, bf16[512,4096]{1,0:T(8,128)(2,1)} %get-tuple-element.9.feat_ref.own_ref, bf16[512,4096]{1,0:T(8,128)(2,1)} %get-tuple-element.11.other_ref), custom_call_target="tpu_custom_call" | custom-call | tf_op jit(solution)/shard_map/pallas_call | solution.py:364

commit v4 on v3

--- a/solution.py
+++ b/solution.py
@@ -208,18 +208,15 @@
 
 
 def feature_kernel(core_ref, emb_ref, freq_ref, phase_ref, sketch_ref, feat_ref, part_ref):
-    mixed = jnp.dot(emb_ref[...], freq_ref[...], preferred_element_type=jnp.float32)
-    value = cosine(mixed + phase_ref[...]).astype(jnp.bfloat16)
-    feat_ref[...] = value
-    term = jnp.dot(value, sketch_ref[...], preferred_element_type=jnp.float32)
-
-    @pl.when(pl.program_id(0) == 0)
-    def _():
-        part_ref[...] = term
-
-    @pl.when(pl.program_id(0) > 0)
-    def _():
-        part_ref[...] += term
+    first = pl.program_id(0) == 0
+    piece = emb_ref.shape[0] // 2
+    for h in range(2):
+        rows = slice(h * piece, (h + 1) * piece)
+        mixed = jnp.dot(emb_ref[rows, :], freq_ref[...], preferred_element_type=jnp.float32)
+        value = cosine(mixed + phase_ref[...]).astype(jnp.bfloat16)
+        feat_ref[rows, :] = value
+        term = jnp.dot(value, sketch_ref[...], preferred_element_type=jnp.float32)
+        part_ref[rows, :] = jnp.where(first, 0.0, part_ref[rows, :]) + term
 
 
 def featurize(core, emb, freqs, phases, sketch, tile=512):
@@ -325,85 +322,83 @@
             work[after:, left:] = work[after:, left:] - update[after - left:, :]
 
 
-def finish_kernel(scale, half, where_ref, sk_ref, own_ref, other_ref, coeff_ref, rows_ref,
-                  work, basis_t, basis, half_t, feats, sem):
-    step = pl.program_id(0)
-    tile = coeff_ref.shape[1]
-    loads = [
-        pltpu.make_async_copy(
+def finish_kernel(scale, half, core_ref, place_ref, sk_ref, own_ref, other_ref, coeff_ref,
+                  rows_ref, work, basis_t, basis, half_t, feats, out, sem, out_sem):
+    tile = out.shape[2]
+    core = core_ref[0]
+    loads, stores = [], []
+    for i in range(2 * half):
+        loads.append(pltpu.make_async_copy(
             (own_ref if i < half else other_ref).at[:, pl.ds(i % half * tile, tile)],
             feats.at[i],
             sem.at[i],
-        )
-        for i in range(2 * half)
-    ]
-
-    @pl.when(step == 0)
-    def _():
-        for load in loads:
-            load.start()
-        factorize(scale, sk_ref, basis_t, work)
-        half_t[...] = basis_t[...].astype(jnp.bfloat16)
-        basis[...] = basis_t[...].T
-        rows = rows_ref.shape[0]
-        rows_ref[...] = basis[pl.ds(pl.multiple_of(where_ref[1] * rows, rows), rows), :]
-
+        ))
+        block = (core if i < half else 1 - core) * half + i % half
+        stores.append(pltpu.make_async_copy(
+            out.at[i],
+            coeff_ref.at[:, pl.ds(pl.multiple_of(block * tile, tile), tile)],
+            out_sem.at[i],
+        ))
+    for load in loads:
+        load.start()
+    factorize(scale, sk_ref, basis_t, work)
+    half_t[...] = basis_t[...].astype(jnp.bfloat16)
     for i in range(2 * half):
-        @pl.when(step == i)
-        def _(i=i):
-            loads[i].wait()
-            coeff_ref[...] = scale * jnp.dot(
-                half_t[...], feats[i], preferred_element_type=jnp.float32
-            )
-
-
-def finish(where, sketched, own, other, rows, tile=1024):
+        loads[i].wait()
+        out[i] = scale * jnp.dot(half_t[...], feats[i], preferred_element_type=jnp.float32)
+        stores[i].start()
+    basis[...] = basis_t[...].T
+    rows = rows_ref.shape[0]
+    rows_ref[...] = basis[pl.ds(pl.multiple_of(place_ref[0] * rows, rows), rows), :]
+    for store in stores:
+        store.wait()
+
+
+def finish(core, place, sketched, own, other, rows, tile=1024):
     total, k = sketched.shape
     width = own.shape[1]
     half = width // tile
     return pl.pallas_call(
         functools.partial(finish_kernel, 1.0 / total, half),
-        grid_spec=pltpu.PrefetchScalarGridSpec(
-            num_scalar_prefetch=1,
-            grid=(2 * half,),
-            in_specs=[
-                pl.BlockSpec((total, k), lambda i, c: (0, 0)),
-                pl.BlockSpec(memory_space=pl.ANY),
-                pl.BlockSpec(memory_space=pl.ANY),
-            ],
-            out_specs=[
-                pl.BlockSpec(
-                    (k, tile),
-                    lambda i, c: (0, jnp.where(i < half, c[0], 1 - c[0]) * half + i % half),
-                ),
-                pl.BlockSpec((rows, k), lambda i, c: (0, 0)),
-            ],
-            scratch_shapes=[
-                pltpu.VMEM((k, k + total), jnp.float32),
-                pltpu.VMEM((k, total), jnp.float32),
-                pltpu.VMEM((total, k), jnp.float32),
-                pltpu.VMEM((k, total), jnp.bfloat16),
-                pltpu.VMEM((2 * half, total, tile), own.dtype),
-                pltpu.SemaphoreType.DMA((2 * half,)),
-            ],
-        ),
+        in_specs=[
+            pl.BlockSpec(memory_space=pltpu.SMEM),
+            pl.BlockSpec(memory_space=pltpu.SMEM),
+            pl.BlockSpec(memory_space=pltpu.VMEM),
+            pl.BlockSpec(memory_space=pl.ANY),
+            pl.BlockSpec(memory_space=pl.ANY),
+        ],
+        out_specs=[
+            pl.BlockSpec(memory_space=pl.ANY),
+            pl.BlockSpec(memory_space=pltpu.VMEM),
+        ],
+        scratch_shapes=[
+            pltpu.VMEM((k, k + total), jnp.float32),
+            pltpu.VMEM((k, total), jnp.float32),
+            pltpu.VMEM((total, k), jnp.float32),
+            pltpu.VMEM((k, total), jnp.bfloat16),
+            pltpu.VMEM((2 * half, total, tile), own.dtype),
+            pltpu.VMEM((2 * half, k, tile), jnp.float32),
+            pltpu.SemaphoreType.DMA((2 * half,)),
+            pltpu.SemaphoreType.DMA((2 * half,)),
+        ],
         out_shape=(
             jax.ShapeDtypeStruct((k, 2 * width), jnp.float32),
             jax.ShapeDtypeStruct((rows, k), jnp.float32),
         ),
         compiler_params=pltpu.CompilerParams(vmem_limit_bytes=60 * MIB),
-    )(where, sketched, own, other)
+    )(core, place, sketched, own, other)
 
 
 def fused(embeddings, freqs, phases, sketch):
     rows_dev = embeddings.shape[0]
     feats, parts = lax.axis_size("feat"), lax.axis_size("rows")
     r, f = lax.axis_index("rows"), lax.axis_index("feat")
-    where = jnp.stack([r % 2, r * feats + f]).astype(jnp.int32)
+    core = jnp.reshape(r % 2, (1,)).astype(jnp.int32)
+    place = jnp.reshape(r * feats + f, (1,)).astype(jnp.int32)
     emb = gather_rows(embeddings, feats, parts)
-    own, partial = featurize(where, emb, freqs, phases, sketch)
+    own, partial = featurize(core, emb, freqs, phases, sketch)
     sketched, other = sum_and_swap(partial, own, feats)
-    coeffs, basis = finish(where, sketched, own, other, rows_dev)
+    coeffs, basis = finish(core, place, sketched, own, other, rows_dev)
     return basis, coeffs
 
 

time: 77.9 us -> 75.6 us (0.970)
  Pallas kernels: 76.1 us -> 74.6 us
where the time goes in v4:
time: 75.6 us; the launch traced here: 75.3 us
  Pallas kernels  74.6 us (99%)
    pallas_call x1, Pallas kernels, sum_and_swap(): pl.pallas_call(functools.partial(sum_kernel, feats), out_shape=(jax.Shape...  21.7 us
    pallas_call x1, Pallas kernels, finish(): pl.pallas_call(functools.partial(finish_kernel, 1.0 / total, half), in_sp...  19.3 us
    pallas_call x1, Pallas kernels, gather_rows(): pl.pallas_call(functools.partial(gather_kernel, feats), out_shape=jax.Sha...  19 us
    pallas_call x1, Pallas kernels, featurize(): pl.pallas_call(feature_kernel, grid_spec=pltpu.PrefetchScalarGridSpec(num...  14.7 us

profile of v4, /device:TPU:0, one launch (start us, length us, event | category | flops | bytes accessed | tf_op | source)
XLA Modules:
  0.0 75.3 jit_solution(12731554135128045483)
XLA Ops:
  0.6 19.0 %shard_map.59.emb_ref = bf16[512,1024]{1,0:T(8,128)(2,1)} custom-call(bf16[16,1024]{1,0:T(8,128)(2,1)} %x_ref.1), custom_call_target="tpu_custom_call" | custom-call | tf_op jit(solution)/shard_map/pallas_call | solution.py:111
  19.6 14.7 %shard_map.60 = (bf16[512,4096]{1,0:T(8,128)(2,1)}, f32[512,256]{1,0:T(8,128)}) custom-call(s32[1]{0:T(128)} %bitcast.core_ref, bf16[512,1024]{1,0:T(8,128)(2,1)} %shard_map.59.emb_ref, bf16[1024,8192]{1,0:T(8,128)(2,1)} %freq_ref.1, f32[1,8192]{1,0:T(1,128)} %bitcast.3, bf16[8192,256]{1,0:T(8,128)(2,1)} %sketch_ref.1), custom_call_target="tpu_custom_call" | custom-call | tf_op jit(solution)/shard_map/pallas_call | solution.py:227
  34.3 21.7 %shard_map.61 = (f32[512,256]{1,0:T(8,128)}, bf16[512,4096]{1,0:T(8,128)(2,1)}) custom-call(f32[512,256]{1,0:T(8,128)} %get-tuple-element.8.part_ref, bf16[512,4096]{1,0:T(8,128)(2,1)} %get-tuple-element.9.feat_ref.own_ref), custom_call_target="tpu_custom_call" | custom-call | tf_op jit(solution)/shard_map/pallas_call | solution.py:179
  56.0 19.3 %shard_map.62 = (f32[256,8192]{1,0:T(8,128)}, f32[16,256]{1,0:T(8,128)}) custom-call(s32[1]{0:T(128)} %bitcast.core_ref, s32[1]{0:T(128)} %bitcast.1.place_ref, f32[512,256]{1,0:T(8,128)} %get-tuple-element.10.sk_ref, bf16[512,4096]{1,0:T(8,128)(2,1)} %get-tuple-element.9.feat_ref.own_ref, bf16[512,4096]{1,0:T(8,128)(2,1)} %get-tuple-element.11.other_ref), custom_call_target="tpu_custom_call" | custom-call | tf_op jit(solution)/shard_map/pallas_call | solution.py:361
